TPU v7x, 32 devices: a whole 2x2x4 slice. The times are simulated.
32 devices in a mesh: wide: 8 (over z, y), narrow: 4 (over x, core).
Axes of the slice: x: 2, y: 2, z: 4, core: 2. Of those that a mesh axis runs over, the one named last changes fastest.
Arguments:
- residual: bfloat16 [8, 4, 2048, 256], P('wide', 'narrow'), may hold values from -6 to 6
- scaling: float32 [8, 4, 2048], P('wide', 'narrow'), may hold values from 0.25 to 1
- local_inverse: bfloat16 [8, 4, 2048, 2048], P('wide', 'narrow'), may hold values from -0.125 to 0.125
- coarse_basis: bfloat16 [8, 4, 24, 2048], P('wide', 'narrow'), may hold values from -0.125 to 0.125
- primal_map: int32 [8, 4, 24], P('wide', 'narrow'), may hold values from 0 to 95
- slot_index: int32 [8, 4, 6, 256], P('wide', 'narrow'), may hold values from 0 to 2047, as said below
- slot_length: int32 [8, 4, 6], P('wide', 'narrow'), may hold values from 0 to 256, as said below
- coarse_sub: float32 [8, 96, 96], P('wide'), may hold values from -0.625 to 0.625
- coarse_pivot: float32 [8, 96, 96], P('wide'), as said below
Outputs:
- interface_sum: float32 [8, 4, 2048, 256], P('wide', 'narrow')
Inputs may be any that keep to these rules, and one draw needn't show every extreme that they name: `slot_index`: within one slot of one subdomain the 256 entries are distinct. `slot_length`: paired slots have equal lengths: slot j of subdomain (w, n) and slot n of (w, j); slot 4 of (w, n) and slot 5 of (w - 1, n). A subdomain's own narrow slot n, the slot 4 of slab 0 and the slot 5 of slab 8 - 1 have length 0. `coarse_pivot`: Symmetric.
All inputs are finite; a program needn't handle non-finite values.
Results may differ from a plain program's by a relative error of at most 0.0039.
The roundings to bfloat16 on the way count: a program that leaves them out, or rounds other values in their place, can miss the bound.
Values may be sent and summed in bfloat16 or wider, within the bound.
No kernel may reach another device: no remote copies, remote signals or barrier semaphores. Data moves between devices by JAX's collectives and lax.ppermute only.
A program may use at most 128 MiB of HBM per device.

v0:
```python
import jax
import jax.numpy as jnp
from jax import lax
from jax.sharding import PartitionSpec as P

highest = lax.Precision.HIGHEST


def entering(part, axis, combine, identity, reverse):
    count = lax.axis_size(axis)
    place = lax.axis_index(axis)
    ahead = count - 1 - place if reverse else place
    gathered = jax.tree.map(lambda a: lax.all_gather(a, axis), part)
    state = jax.tree.map(lambda a, e: jnp.zeros_like(a) + jnp.asarray(e, a.dtype), part, identity)

    def one(turn, state):
        source = count - 1 - turn if reverse else turn
        return combine(
            state, jax.tree.map(lambda a: lax.dynamic_index_in_dim(a, source, 0, False), gathered)
        )

    return lax.fori_loop(0, ahead, one, state)


def shifted(block, axis, distance):
    devices = range(lax.axis_size(axis))
    route = [(i - distance, i) for i in devices if i - distance in devices]
    return lax.ppermute(block, axis, route)


def exact_dot(left, right):
    return jnp.dot(left, right, precision=highest, preferred_element_type=jnp.float32)


def compose(earlier, later):
    return (exact_dot(later[0], earlier[0]), exact_dot(later[0], earlier[1]) + later[1])


def coarse_solve(coarse_rhs, sub_block, pivot_block):
    order = sub_block.shape[0]
    identity = jnp.eye(order, dtype=jnp.float32)
    empty = jnp.zeros_like(coarse_rhs)
    sub_trans = sub_block.T
    before = entering((-sub_block, coarse_rhs), "wide", compose, (identity, empty), False)
    chain_y = coarse_rhs - exact_dot(sub_block, before[1])
    pivoted = exact_dot(pivot_block, chain_y)
    after = entering(
        (-sub_trans, exact_dot(sub_trans, pivoted)), "wide", compose, (identity, empty), True
    )
    return pivoted - after[1]


def body(
    residual,
    scaling,
    local_inverse,
    coarse_basis,
    primal_map,
    slot_index,
    slot_length,
    coarse_sub,
    coarse_pivot,
):
    groups = lax.axis_size("narrow")
    weights = scaling[0, 0]
    weighted = (weights[:, None] * residual[0, 0].astype(jnp.float32)).astype(jnp.bfloat16)
    local_part = jnp.dot(local_inverse[0, 0], weighted, preferred_element_type=jnp.float32)
    basis = coarse_basis[0, 0]
    primal = jnp.dot(basis, weighted, preferred_element_type=jnp.float32)
    order = coarse_sub.shape[1]
    one_hot = (primal_map[0, 0][:, None] == jnp.arange(order, dtype=jnp.int32)[None, :]).astype(
        jnp.float32
    )
    assembly = lax.dot_general(
        one_hot,
        primal,
        (((0,), (0,)), ((), ())),
        precision=highest,
        preferred_element_type=jnp.float32,
    )
    coarse_share = lax.psum_scatter(assembly, "narrow", scatter_dimension=1, tiled=True)
    solved_share = coarse_solve(coarse_share, coarse_sub[0], coarse_pivot[0])
    coarse_sol = lax.all_gather(solved_share, "narrow", axis=1, tiled=True)
    coarse_vals = exact_dot(one_hot, coarse_sol)
    spread = lax.dot_general(
        basis.astype(jnp.float32),
        coarse_vals,
        (((0,), (0,)), ((), ())),
        precision=highest,
        preferred_element_type=jnp.float32,
    )
    combined = (weights[:, None] * (local_part + spread)).astype(jnp.bfloat16)
    indices = slot_index[0, 0]
    lengths = slot_length[0, 0]
    capacity = indices.shape[1]
    live_mask = jnp.arange(capacity, dtype=jnp.int32)[None, :] < lengths[:, None]
    outgoing = jnp.where(live_mask[:, :, None], combined[indices], jnp.zeros((), jnp.bfloat16))
    narrow_in = lax.all_to_all(outgoing[:groups], "narrow", split_axis=0, concat_axis=0, tiled=True)
    below = shifted(outgoing[groups + 1], "wide", 1)
    above = shifted(outgoing[groups], "wide", -1)
    incoming = jnp.concatenate([narrow_in, below[None], above[None]], axis=0)
    columns = combined.shape[1]
    summed = (
        combined.astype(jnp.float32)
        .at[indices.reshape(-1)]
        .add(incoming.reshape(-1, columns).astype(jnp.float32))
    )
    return summed[None, None]


def solution(mesh):
    in_specs = (
        P("wide", "narrow", None, None),
        P("wide", "narrow", None),
        P("wide", "narrow", None, None),
        P("wide", "narrow", None, None),
        P("wide", "narrow", None),
        P("wide", "narrow", None, None),
        P("wide", "narrow", None),
        P("wide", None, None),
        P("wide", None, None),
    )
    out_specs = P("wide", "narrow", None, None)
    return jax.shard_map(body, mesh=mesh, in_specs=in_specs, out_specs=out_specs, check_vma=False)
```

profile of v0, /device:TPU:0, one launch (start us, length us, event | category | flops | bytes accessed | tf_op | source)
XLA Modules:
  0.0 194.7 jit_solution(11893826487892499667)
XLA Ops:
  6.5 0.0 copy-start
  6.5 0.0 copy-start.4
  6.5 0.0 reduce-scatter.2.cloned.1.call-start
  6.6 0.9 copy-done
  7.5 2.1 %fusion.15 = f32[256,24]{1,0:T(8,128)S(1)} fusion(bf16[1,1,2048,256]{3,2,1,0:T(8,128)(2,1)} %param.13, f32[2048]{0:T(1024)} %bitcast.94, bf16[1,1,24,2048]{3,2,1,0:T(8,128)(2,1)S(1)} %copy-done), kind=kOutput, calls=%fused_computation.25 | convolution fusion | flops 26738688 | bytes 1179648 | tf_op jit(solution)/shard_map/dot_general | solution.py:69
  9.5 1.6 fusion.26
  11.1 0.0 reduce-scatter.2.cloned.1.call-update
  11.1 0.0 copy-done.1
  11.1 0.1 copy.13
  11.2 0.0 copy-done.3
  11.3 32.9 %all_gather.25 = f32[8,96,96]{2,1,0:T(8,128)S(1)} all-gather(f32[1,96,96]{2,1,0:T(8,128)S(1)} %neg.10), channel_id=1, replica_groups=mesh['wide'=8,'narrow'=4] {'wide'}, dimensions={0}, use_global_device_ids=true | all-gather | bytes 331776 | tf_op jit(solution)/shard_map/all_gather | solution.py:13
  44.3 30.9 %all-gather.1 = f32[768,96]{1,0:T(8,128)S(1)} all-gather(f32[96,96]{1,0:T(8,128)S(1)} %fusion.24), channel_id=3, replica_groups=mesh['wide'=8,'narrow'=4] {'wide'}, dimensions={0}, use_global_device_ids=true | all-gather | bytes 331776 | tf_op jit(solution)/shard_map/all_gather | solution.py:13
  75.2 0.0 copy-done.4
  75.2 6.5 %fusion.6 = f32[256,2048]{1,0:T(8,128)S(1)} fusion(bf16[1,1,2048,2048]{3,2,1,0:T(8,128)(2,1)} %param.15, bf16[1,1,2048,256]{3,2,1,0:T(8,128)(2,1)} %param.13, f32[2048]{0:T(1024)S(1)} %bitcast.95), kind=kOutput, calls=%fused_computation.10 | convolution fusion | flops 2149056512 | bytes 11542528 | tf_op jit(solution)/shard_map/dot_general | solution.py:67
  81.7 0.0 copy-start.5
  81.7 0.0 copy-done.6
  81.7 0.1 iota_compare_fusion.3
  81.8 30.9 %all-gather.3 = f32[8,96,64]{1,2,0:T(8,128)S(1)} all-gather(f32[1,96,64]{1,2,0:T(8,128)} %bitcast.92), channel_id=2, replica_groups=mesh['wide'=8,'narrow'=4] {'wide'}, dimensions={0}, use_global_device_ids=true | all-gather | bytes 221184 | tf_op jit(solution)/shard_map/all_gather | solution.py:13
  112.7 1.0 fusion.13
  113.7 0.0 copy-done.2
  113.7 0.2 fusion.22
  114.0 0.2 convolution_bitcast_fusion
  114.1 32.2 %all-gather.4 = f32[8,96,64]{1,2,0:T(8,128)S(1)} all-gather(f32[1,96,64]{1,2,0:T(8,128)S(1)} %convolution_bitcast_fusion), channel_id=4, replica_groups=mesh['wide'=8,'narrow'=4] {'wide'}, dimensions={0}, use_global_device_ids=true | all-gather | bytes 221184 | tf_op jit(solution)/shard_map/all_gather | solution.py:13
  146.4 1.8 while.27
  146.4 0.2 convolution_add_fusion.6
  146.6 0.2 convolution_add_fusion.6
  146.9 0.2 convolution_add_fusion.6
  147.1 0.2 convolution_add_fusion.6
  147.4 0.2 convolution_add_fusion.6
  147.7 0.2 convolution_add_fusion.6
  147.9 0.2 convolution_add_fusion.6
  148.2 5.4 %all_gather.32 = f32[96,256]{0,1:T(8,128)S(1)} all-gather(f32[96,64]{0,1:T(8,128)S(1)} %bitcast_subtract_fusion), channel_id=1, replica_groups=mesh['wide'=8,'narrow'=4] {'narrow'}, dimensions={1}, use_global_device_ids=true | all-gather | bytes 122880 | tf_op jit(solution)/shard_map/all_gather | solution.py:83
  153.6 0.0 copy-done.5
  153.6 0.2 fusion.25
  153.8 1.2 fusion.10
  155.0 0.5 copy.14
  155.5 4.8 %gather_fusion = bf16[1536,256]{1,0:T(8,128)(2,1)S(1)} fusion(bf16[2048,256]{1,0:T(8,128)(2,1)S(1)} %copy.14, s32[2048]{0:T(1024)S(1)} %pad_clamp_fusion), kind=kCustom, calls=%fused_computation | custom fusion | bytes 1579008 | tf_op jit(solution)/shard_map/gather | solution.py:97
  160.3 0.3 broadcast_select_fusion
  160.6 0.8 slice.14
  161.4 3.5 %all-to-all-start = ((bf16[4,256,256]{2,1,0:T(8,128)(2,1)}), bf16[4,256,256]{2,1,0:T(8,128)(2,1)S(1)}, u32[]{:S(2)}, u32[]{:S(2)}) async-start(bf16[4,256,256]{2,1,0:T(8,128)(2,1)} %slice.14), calls=%async_computation.1 | async-start | bytes 1048576 | tf_op jit(solution)/shard_map/all_to_all | solution.py:98
  164.9 3.7 %collective-permute-start = (bf16[256,256]{1,0:T(8,128)(2,1)S(1)}, bf16[256,256]{1,0:T(8,128)(2,1)S(1)}, u32[]{:S(2)}, u32[]{:S(2)}) collective-permute-start(bf16[256,256]{1,0:T(8,128)(2,1)S(1)} %get-tuple-element.155), channel_id=1, source_target_pairs={{0,4},{4,8},{8,12},{12,16},{16,20},{20,24},{24,28},{1,5},{5,9},{9,... | collective-permute-start | bytes 393224 | tf_op jit(solution)/shard_map/ppermute | solution.py:28
  168.6 1.3 collective-permute-start.1
  169.9 1.6 copy.15
  171.5 0.4 collective-permute-done
  171.9 4.1 %collective-permute-done.1 = bf16[256,256]{1,0:T(8,128)(2,1)S(1)} collective-permute-done((bf16[256,256]{1,0:T(8,128)(2,1)S(1)}, bf16[256,256]{1,0:T(8,128)(2,1)S(1)}, u32[]{:S(2)}, u32[]{:S(2)}) %collective-permute-start.1) | collective-permute-done | bytes 131104 | tf_op jit(solution)/shard_map/ppermute | solution.py:28
  176.1 0.0 all-to-all-done
  176.1 0.1 pad_maximum_fusion
  176.2 11.7 %scatter_custom_fusion = f32[2048,256]{1,0:T(8,128)} fusion(f32[2048,256]{1,0:T(8,128)} %copy.15, s32[1536]{0:T(1024)S(1)} %fusion.27, bf16[1536,256]{1,0:T(8,128)(2,1)S(1)} %bitcast.87), kind=kCustom, calls=%fused_computation.17 | custom fusion | flops 786432 | bytes 2883584 | tf_op jit(solution)/shard_map/scatter-add | solution.py:106
  (23 shorter events, 0.1 us)
Async XLA Ops:
  6.5 0.9 copy-start
  6.5 68.7 %copy-start.4 = (f32[1,1,2048]{2,1,0:T(1,128)S(1)}, f32[1,1,2048]{2,1,0:T(1,128)}, u32[]{:S(2)}) copy-start(f32[1,1,2048]{2,1,0:T(1,128)} %param.14) | copy-start | bytes 24580
  6.5 4.6 %copy-start.1 = (f32[1,96,96]{2,1,0:T(8,128)S(1)}, f32[1,96,96]{2,1,0:T(8,128)}, u32[]{:S(2)}) copy-start(f32[1,96,96]{2,1,0:T(8,128)} %param.20) | copy-start | bytes 110596
  6.5 4.7 %copy-start.3 = (s32[1,1,6,256]{3,1,2,0:T(1,128)S(1)}, s32[1,1,6,256]{3,1,2,0:T(1,128)}, u32[]{:S(2)}) copy-start(s32[1,1,6,256]{3,1,2,0:T(1,128)} %param.18) | copy-start | bytes 18436
  6.5 75.3 %reduce-scatter.2.cloned.1.call-start = ((), (), s32[]{:S(2)}) async-start(), calls=%async_computation.2 | async-start | bytes 163840 | tf_op jit(solution)/shard_map/reduce_scatter | solution.py:81
  75.2 6.5 %copy-start.6 = (s32[1,1,6]{2,1,0:T(1,128)S(1)}, s32[1,1,6]{2,1,0:T(1,128)}, u32[]{:S(2)}) copy-start(s32[1,1,6]{2,1,0:T(1,128)} %param.19) | copy-start | bytes 76
  75.2 38.5 %copy-start.2 = (f32[1,96,96]{2,1,0:T(8,128)S(1)}, f32[1,96,96]{2,1,0:T(8,128)}, u32[]{:S(2)}) copy-start(f32[1,96,96]{2,1,0:T(8,128)} %param.21) | copy-start | bytes 110596
  81.7 71.9 %copy-start.5 = (s32[1,1,24]{2,1,0:T(1,128)S(1)}, s32[1,1,24]{2,1,0:T(1,128)}, u32[]{:S(2)}) copy-start(s32[1,1,24]{2,1,0:T(1,128)} %param.17) | copy-start | bytes 292
  161.4 14.7 %all-to-all-start = ((bf16[4,256,256]{2,1,0:T(8,128)(2,1)}), bf16[4,256,256]{2,1,0:T(8,128)(2,1)S(1)}, u32[]{:S(2)}, u32[]{:S(2)}) async-start(bf16[4,256,256]{2,1,0:T(8,128)(2,1)} %slice.14), calls=%async_computation.1 | async-start | bytes 1048576 | tf_op jit(solution)/shard_map/all_to_all | solution.py:98
  164.9 7.0 %collective-permute-start = (bf16[256,256]{1,0:T(8,128)(2,1)S(1)}, bf16[256,256]{1,0:T(8,128)(2,1)S(1)}, u32[]{:S(2)}, u32[]{:S(2)}) collective-permute-start(bf16[256,256]{1,0:T(8,128)(2,1)S(1)} %get-tuple-element.155), channel_id=1, source_target_pairs={{0,4},{4,8},{8,12},{12,16},{16,20},{20,24},{24,28},{1,5},{5,9},{9,... | collective-permute-start | bytes 393224 | tf_op jit(solution)/shard_map/ppermute | solution.py:28
  168.6 7.5 %collective-permute-start.1 = (bf16[256,256]{1,0:T(8,128)(2,1)S(1)}, bf16[256,256]{1,0:T(8,128)(2,1)S(1)}, u32[]{:S(2)}, u32[]{:S(2)}) collective-permute-start(bf16[256,256]{1,0:T(8,128)(2,1)S(1)} %get-tuple-element.156), channel_id=1, source_target_pairs={{4,0},{8,4},{12,8},{16,12},{20,16},{24,20},{28,24},{5,1},{9,5},{13... | collective-permute-start | bytes 393224 | tf_op jit(solution)/shard_map/ppermute | solution.py:28
Sparse Core Ops, SparseCore 0:
  11.2 22.3 reduce-scatter.1
where the time goes:
time: 195 us
  blocking collectives  132 us (68%)
  matrix products  14.4 us (7%)
  between operations  13.6 us (7%)
  other arithmetic  12.2 us (6%)
  local copies, waits for them, and re-layouts  8.77 us (4%)
  starting transfers between devices  8.46 us (4%)
  waiting for transfers between devices  4.55 us (2%)
    all_gather x4, blocking collectives, entering(): gathered = jax.tree.map(lambda a: lax.all_gather(a, axis), part)  127 us
    scatter-add x1, other arithmetic, body(): summed = combined.astype(jnp.float32).at[indices.reshape(-1)].add(incomin...  11.7 us
    dot_general x1, matrix products, body(): jnp.dot(local_inverse[0, 0], weighted, preferred_element_type=jnp.float32)  6.48 us
    all_gather x1, blocking collectives, body(): coarse_sol = lax.all_gather(solved_share, 'narrow', axis=1, tiled=True)  5.42 us
    ppermute x2, starting transfers between devices, shifted(): return lax.ppermute(block, axis, route)  4.95 us
    gather x1, local copies, waits for them, and re-layouts, body(): combined[indices]  4.76 us
    ppermute x2, waiting for transfers between devices, shifted(): return lax.ppermute(block, axis, route)  4.53 us
  transfers between devices with their start and end apart: 4, of which 2 were waited for; matrix products, arithmetic and copies ran while one was open for 4% of the time, Pallas kernels for 0%

commit v1 on v0

--- a/solution.py
+++ b/solution.py
@@ -80,7 +80,9 @@
     )
     coarse_share = lax.psum_scatter(assembly, "narrow", scatter_dimension=1, tiled=True)
     solved_share = coarse_solve(coarse_share, coarse_sub[0], coarse_pivot[0])
-    coarse_sol = lax.all_gather(solved_share, "narrow", axis=1, tiled=True)
+    coarse_sol = jnp.concatenate(
+        lax.all_to_all(jnp.stack([solved_share] * lax.axis_size("narrow")), "narrow", 0, 0), axis=1
+    )
     coarse_vals = exact_dot(one_hot, coarse_sol)
     spread = lax.dot_general(
         basis.astype(jnp.float32),

time: 195 us -> 200 us (1.026)
  blocking collectives: 132 us -> 127 us
  waiting for transfers between devices: 4.55 us -> 9.09 us
  starting transfers between devices: 8.46 us -> 11.8 us
    all_gather x1 -> x0, blocking collectives: 5.42 us -> none  [body(): coarse_sol = lax.all_gather(solved_share, 'narrow', axis=1, tiled=True)]
    all_to_all x0 -> x1, waiting for transfers between devices: none -> 4.55 us  [body(): lax.all_to_all(jnp.stack([solved_share] * lax.axis_size('narrow')), 'narr...]
    all_to_all x0 -> x1, starting transfers between devices: none -> 3.33 us  [body(): lax.all_to_all(jnp.stack([solved_share] * lax.axis_size('narrow')), 'narr...]
  transfers between devices with their start and end apart: 4 -> 5, of which waited for: 2 -> 3; matrix products, arithmetic and copies ran while one was open for 4% -> 5% of each run, Pallas kernels for 0% -> 0%
where the time goes in v1:
time: 200 us
  blocking collectives  127 us (64%)
  matrix products  14 us (7%)
  other arithmetic  13.7 us (7%)
  between operations  13.6 us (7%)
  starting transfers between devices  11.8 us (6%)
  local copies, waits for them, and re-layouts  10.2 us (5%)
  waiting for transfers between devices  9.09 us (5%)
    all_gather x4, blocking collectives, entering(): gathered = jax.tree.map(lambda a: lax.all_gather(a, axis), part)  127 us
    scatter-add x1, other arithmetic, body(): summed = combined.astype(jnp.float32).at[indices.reshape(-1)].add(incomin...  11.7 us
    dot_general x1, matrix products, body(): jnp.dot(local_inverse[0, 0], weighted, preferred_element_type=jnp.float32)  6.5 us
    ppermute x2, starting transfers between devices, shifted(): return lax.ppermute(block, axis, route)  4.96 us
    gather x1, local copies, waits for them, and re-layouts, body(): combined[indices]  4.76 us
    all_to_all x1, waiting for transfers between devices, body(): lax.all_to_all(jnp.stack([solved_share] * lax.axis_size('narrow')), 'narr...  4.55 us
    ppermute x2, waiting for transfers between devices, shifted(): return lax.ppermute(block, axis, route)  4.52 us
  transfers between devices with their start and end apart: 5, of which 3 were waited for; matrix products, arithmetic and copies ran while one was open for 5% of the time, Pallas kernels for 0%

profile of v1, /device:TPU:0, one launch (start us, length us, event | category | flops | bytes accessed | tf_op | source)
XLA Modules:
  0.0 199.7 jit_solution(13801341635899596348)
XLA Ops:
  6.5 0.0 copy-start
  6.5 0.9 copy-done
  7.4 1.7 fusion.15
  9.1 1.6 fusion.26
  10.7 0.0 reduce-scatter.2.cloned.1.call-update
  10.8 0.9 copy.17
  11.6 0.8 neg.10
  12.5 0.7 fusion.28
  13.2 32.9 %all_gather.22 = f32[8,96,96]{2,1,0:T(8,128)S(1)} all-gather(f32[1,96,96]{2,1,0:T(8,128)S(1)} %neg.10), channel_id=1, replica_groups=mesh['wide'=8,'narrow'=4] {'wide'}, dimensions={0}, use_global_device_ids=true | all-gather | bytes 331776 | tf_op jit(solution)/shard_map/all_gather | solution.py:13
  46.1 30.9 %all-gather.1 = f32[768,96]{1,0:T(8,128)S(1)} all-gather(f32[96,96]{1,0:T(8,128)S(1)} %fusion.24), channel_id=3, replica_groups=mesh['wide'=8,'narrow'=4] {'wide'}, dimensions={0}, use_global_device_ids=true | all-gather | bytes 331776 | tf_op jit(solution)/shard_map/all_gather | solution.py:13
  77.1 0.0 copy-start.2
  77.1 6.5 %fusion.6 = f32[256,2048]{1,0:T(8,128)S(1)} fusion(bf16[1,1,2048,2048]{3,2,1,0:T(8,128)(2,1)} %param.15, bf16[1,1,2048,256]{3,2,1,0:T(8,128)(2,1)} %param.13, f32[2048]{0:T(1024)S(1)} %bitcast.99), kind=kOutput, calls=%fused_computation.10 | convolution fusion | flops 2149056512 | bytes 11542528 | tf_op jit(solution)/shard_map/dot_general | solution.py:67
  83.6 0.0 copy-start.5
  83.6 0.1 iota_compare_fusion.3
  83.7 30.9 %all-gather.3 = f32[8,96,64]{1,2,0:T(8,128)S(1)} all-gather(f32[1,96,64]{1,2,0:T(8,128)} %bitcast.96), channel_id=2, replica_groups=mesh['wide'=8,'narrow'=4] {'wide'}, dimensions={0}, use_global_device_ids=true | all-gather | bytes 221184 | tf_op jit(solution)/shard_map/all_gather | solution.py:13
  114.7 0.0 copy-done.1
  114.7 1.0 fusion.13
  115.6 0.0 copy-done.2
  115.7 0.2 fusion.22
  115.9 0.2 convolution_bitcast_fusion
  116.1 32.2 %all-gather.4 = f32[8,96,64]{1,2,0:T(8,128)S(1)} all-gather(f32[1,96,64]{1,2,0:T(8,128)S(1)} %convolution_bitcast_fusion), channel_id=4, replica_groups=mesh['wide'=8,'narrow'=4] {'wide'}, dimensions={0}, use_global_device_ids=true | all-gather | bytes 221184 | tf_op jit(solution)/shard_map/all_gather | solution.py:13
  148.2 1.8 while.27
  148.2 0.2 convolution_add_fusion.6
  148.5 0.2 convolution_add_fusion.6
  148.8 0.2 convolution_add_fusion.6
  149.0 0.2 convolution_add_fusion.6
  149.3 0.2 convolution_add_fusion.6
  149.5 0.2 convolution_add_fusion.6
  149.8 0.2 convolution_add_fusion.6
  150.1 0.7 stack.2
  150.7 3.3 %all-to-all-start = ((f32[4,96,64]{1,2,0:T(8,128)}), f32[4,96,64]{1,2,0:T(8,128)S(1)}, u32[]{:S(2)}, u32[]{:S(2)}) async-start(f32[4,96,64]{1,2,0:T(8,128)} %stack.2), calls=%async_computation.1 | async-start | bytes 262144 | tf_op jit(solution)/shard_map/all_to_all | solution.py:84
  154.1 4.6 %all-to-all-done = f32[4,96,64]{1,2,0:T(8,128)S(1)} async-done(((f32[4,96,64]{1,2,0:T(8,128)}), f32[4,96,64]{1,2,0:T(8,128)S(1)}, u32[]{:S(2)}, u32[]{:S(2)}) %all-to-all-start) | async-done | bytes 98336 | tf_op jit(solution)/shard_map/all_to_all | solution.py:84
  158.6 0.2 fusion.25
  158.8 1.1 fusion.10
  160.0 0.5 copy.18
  160.5 4.8 %gather_fusion = bf16[1536,256]{1,0:T(8,128)(2,1)S(1)} fusion(bf16[2048,256]{1,0:T(8,128)(2,1)S(1)} %copy.18, s32[2048]{0:T(1024)S(1)} %pad_clamp_fusion), kind=kCustom, calls=%fused_computation | custom fusion | bytes 1579008 | tf_op jit(solution)/shard_map/gather | solution.py:99
  165.3 0.0 copy-start.3
  165.3 0.3 broadcast_select_fusion
  165.6 0.8 slice.14
  166.4 3.5 %all-to-all-start.1 = ((bf16[4,256,256]{2,1,0:T(8,128)(2,1)}), bf16[4,256,256]{2,1,0:T(8,128)(2,1)S(1)}, u32[]{:S(2)}, u32[]{:S(2)}) async-start(bf16[4,256,256]{2,1,0:T(8,128)(2,1)} %slice.14), calls=%async_computation.2 | async-start | bytes 1048576 | tf_op jit(solution)/shard_map/all_to_all | solution.py:100
  169.9 3.7 %collective-permute-start = (bf16[256,256]{1,0:T(8,128)(2,1)S(1)}, bf16[256,256]{1,0:T(8,128)(2,1)S(1)}, u32[]{:S(2)}, u32[]{:S(2)}) collective-permute-start(bf16[256,256]{1,0:T(8,128)(2,1)S(1)} %get-tuple-element.155), channel_id=1, source_target_pairs={{0,4},{4,8},{8,12},{12,16},{16,20},{20,24},{24,28},{1,5},{5,9},{9,... | collective-permute-start | bytes 393224 | tf_op jit(solution)/shard_map/ppermute | solution.py:28
  173.6 1.3 collective-permute-start.1
  174.9 1.6 copy.19
  176.5 0.4 collective-permute-done
  176.9 4.1 %collective-permute-done.1 = bf16[256,256]{1,0:T(8,128)(2,1)S(1)} collective-permute-done((bf16[256,256]{1,0:T(8,128)(2,1)S(1)}, bf16[256,256]{1,0:T(8,128)(2,1)S(1)}, u32[]{:S(2)}, u32[]{:S(2)}) %collective-permute-start.1) | collective-permute-done | bytes 131104 | tf_op jit(solution)/shard_map/ppermute | solution.py:28
  181.0 0.0 all-to-all-done.1
  181.1 0.1 pad_maximum_fusion
  181.2 11.7 %scatter_custom_fusion = f32[2048,256]{1,0:T(8,128)} fusion(f32[2048,256]{1,0:T(8,128)} %copy.19, s32[1536]{0:T(1024)S(1)} %fusion.27, bf16[1536,256]{1,0:T(8,128)(2,1)S(1)} %bitcast.90), kind=kCustom, calls=%fused_computation.17 | custom fusion | flops 786432 | bytes 2883584 | tf_op jit(solution)/shard_map/scatter-add | solution.py:108
  (25 shorter events, 0.1 us)
Async XLA Ops:
  6.5 0.9 copy-start
  6.5 70.5 %copy-start.4 = (f32[1,1,2048]{2,1,0:T(1,128)S(1)}, f32[1,1,2048]{2,1,0:T(1,128)}, u32[]{:S(2)}) copy-start(f32[1,1,2048]{2,1,0:T(1,128)} %param.14) | copy-start | bytes 24580
  6.5 77.2 %reduce-scatter.2.cloned.1.call-start = ((), (), s32[]{:S(2)}) async-start(), calls=%async_computation.3 | async-start | bytes 163840 | tf_op jit(solution)/shard_map/reduce_scatter | solution.py:81
  77.1 6.5 %copy-start.6 = (s32[1,1,6]{2,1,0:T(1,128)S(1)}, s32[1,1,6]{2,1,0:T(1,128)}, u32[]{:S(2)}) copy-start(s32[1,1,6]{2,1,0:T(1,128)} %param.19) | copy-start | bytes 76
  77.1 37.6 %copy-start.1 = (f32[1,96,96]{2,1,0:T(8,128)S(1)}, f32[1,96,96]{2,1,0:T(8,128)}, u32[]{:S(2)}) copy-start(f32[1,96,96]{2,1,0:T(8,128)} %param.20) | copy-start | bytes 110596
  77.1 38.6 %copy-start.2 = (f32[1,96,96]{2,1,0:T(8,128)S(1)}, f32[1,96,96]{2,1,0:T(8,128)}, u32[]{:S(2)}) copy-start(f32[1,96,96]{2,1,0:T(8,128)} %param.21) | copy-start | bytes 110596
  83.6 75.0 %copy-start.5 = (s32[1,1,24]{2,1,0:T(1,128)S(1)}, s32[1,1,24]{2,1,0:T(1,128)}, u32[]{:S(2)}) copy-start(s32[1,1,24]{2,1,0:T(1,128)} %param.17) | copy-start | bytes 292
  150.7 7.9 %all-to-all-start = ((f32[4,96,64]{1,2,0:T(8,128)}), f32[4,96,64]{1,2,0:T(8,128)S(1)}, u32[]{:S(2)}, u32[]{:S(2)}) async-start(f32[4,96,64]{1,2,0:T(8,128)} %stack.2), calls=%async_computation.1 | async-start | bytes 262144 | tf_op jit(solution)/shard_map/all_to_all | solution.py:84
  165.3 9.6 %copy-start.3 = (s32[1,1,6,256]{3,1,2,0:T(1,128)S(1)}, s32[1,1,6,256]{3,1,2,0:T(1,128)}, u32[]{:S(2)}) copy-start(s32[1,1,6,256]{3,1,2,0:T(1,128)} %param.18) | copy-start | bytes 18436
  166.4 14.7 %all-to-all-start.1 = ((bf16[4,256,256]{2,1,0:T(8,128)(2,1)}), bf16[4,256,256]{2,1,0:T(8,128)(2,1)S(1)}, u32[]{:S(2)}, u32[]{:S(2)}) async-start(bf16[4,256,256]{2,1,0:T(8,128)(2,1)} %slice.14), calls=%async_computation.2 | async-start | bytes 1048576 | tf_op jit(solution)/shard_map/all_to_all | solution.py:100
  169.9 7.0 %collective-permute-start = (bf16[256,256]{1,0:T(8,128)(2,1)S(1)}, bf16[256,256]{1,0:T(8,128)(2,1)S(1)}, u32[]{:S(2)}, u32[]{:S(2)}) collective-permute-start(bf16[256,256]{1,0:T(8,128)(2,1)S(1)} %get-tuple-element.155), channel_id=1, source_target_pairs={{0,4},{4,8},{8,12},{12,16},{16,20},{20,24},{24,28},{1,5},{5,9},{9,... | collective-permute-start | bytes 393224 | tf_op jit(solution)/shard_map/ppermute | solution.py:28
  173.6 7.5 %collective-permute-start.1 = (bf16[256,256]{1,0:T(8,128)(2,1)S(1)}, bf16[256,256]{1,0:T(8,128)(2,1)S(1)}, u32[]{:S(2)}, u32[]{:S(2)}) collective-permute-start(bf16[256,256]{1,0:T(8,128)(2,1)S(1)} %get-tuple-element.156), channel_id=1, source_target_pairs={{4,0},{8,4},{12,8},{16,12},{20,16},{24,20},{28,24},{5,1},{9,5},{13... | collective-permute-start | bytes 393224 | tf_op jit(solution)/shard_map/ppermute | solution.py:28
Sparse Core Ops, SparseCore 0:
  10.9 22.3 reduce-scatter.1
